TPU v7x, 32 devices: a whole 2x2x4 slice. The times are simulated.
32 devices in a mesh: tm: 8 (over y, x, core), space: 4 (over z).
Axes of the slice: x: 2, y: 2, z: 4, core: 2. Of those that a mesh axis runs over, the one named last changes fastest.
Arguments:
- frames: bfloat16 [128, 256, 768], P('tm', 'space'), may hold values from -6 to 6
- gain_time: float32 [768], replicated, may hold values from 0.25 to 1.75
- wq_time: bfloat16 [768, 768], replicated, may hold values from -6 to 6
- wkv_time: bfloat16 [768, 512], replicated, may hold values from -6 to 6
- wo_time: bfloat16 [768, 768], replicated, may hold values from -0.21875 to 0.21875
- gain_space: float32 [768], replicated, may hold values from 0.25 to 1.75
- wq_space: bfloat16 [768, 768], replicated, may hold values from -6 to 6
- wkv_space: bfloat16 [768, 512], replicated, may hold values from -6 to 6
- wo_space: bfloat16 [768, 768], replicated, may hold values from -0.21875 to 0.21875
- gain_mlp: float32 [768], replicated, may hold values from 0.25 to 1.75
- w_in: bfloat16 [768, 3072], replicated, may hold values from -0.21875 to 0.21875
- w_out: bfloat16 [3072, 768], replicated, may hold values from -0.109375 to 0.109375
Outputs:
- encoded: bfloat16 [128, 256, 768], P('tm', 'space')
All inputs are finite; a program needn't handle non-finite values.
Results may differ from a plain program's by a relative error of at most 0.025.
The roundings to bfloat16 on the way count: a program that leaves them out, or rounds other values in their place, can miss the bound.
Values may be sent and summed in bfloat16 or wider, within the bound.
A program may use at most 192 MiB of HBM per device.

v0:
```python
import jax
import jax.numpy as jnp
from jax import lax
from jax.sharding import PartitionSpec as P

HEADS = 12
KV_HEADS = 4
HEAD = 64
WINDOW = 8


def extended(x, sides, width):
    for axis, dim in sides:
        size, length = (lax.axis_size(axis), x.shape[dim])
        up = [(i, (i + 1) % size) for i in range(size - 1)]
        down = [(j, i) for i, j in up]
        last = lax.slice_in_dim(x, length - width, length, axis=dim)
        leading = lax.slice_in_dim(x, 0, width, axis=dim)
        before = lax.ppermute(last, axis, up)
        after = lax.ppermute(leading, axis, down)
        x = jnp.concatenate([before, x, after], axis=dim)
    return x


def layer_norm(x, gain):
    xf = x.astype(jnp.float32)
    mean = jnp.mean(xf, axis=-1, keepdims=True)
    var = jnp.mean((xf - mean) * (xf - mean), axis=-1, keepdims=True)
    return ((xf - mean) * lax.rsqrt(var + 1e-06) * gain).astype(jnp.bfloat16)


def project(a, w):
    flat = a.reshape(-1, a.shape[-1])
    return jnp.dot(flat, w, preferred_element_type=jnp.float32).reshape(
        a.shape[:-1] + (w.shape[1],)
    )


def banded_time(queries, padded, valid):
    group = HEADS // KV_HEADS
    count = queries.shape[0]
    patches = queries.shape[1]
    extent = padded.shape[0]
    q_heads = queries.reshape(count, patches, KV_HEADS, group, HEAD)
    k_heads = padded[..., : KV_HEADS * HEAD].reshape(extent, patches, KV_HEADS, HEAD)
    v_heads = padded[..., KV_HEADS * HEAD :].reshape(extent, patches, KV_HEADS, HEAD)
    scores = jnp.einsum(
        "tpgrd,spgd->pgtrs", q_heads, k_heads, preferred_element_type=jnp.float32
    ) / jnp.sqrt(jnp.float32(HEAD))
    scores = jnp.where(valid[:, None, :], scores, jnp.float32(-1e30))
    top = jnp.max(scores, axis=-1, keepdims=True)
    expo = jnp.exp(scores - top)
    weights = (expo / jnp.sum(expo, axis=-1, keepdims=True)).astype(jnp.bfloat16)
    out = jnp.einsum("pgtrs,spgd->tpgrd", weights, v_heads, preferred_element_type=jnp.float32)
    return out.reshape(count, patches, HEADS * HEAD).astype(jnp.bfloat16)


def attend_space(query, keyvals):
    group = HEADS // KV_HEADS
    patches = query.shape[0]
    count = keyvals.shape[0]
    q_heads = query.reshape(patches, KV_HEADS, group, HEAD)
    k_heads = keyvals[:, : KV_HEADS * HEAD].reshape(count, KV_HEADS, HEAD)
    v_heads = keyvals[:, KV_HEADS * HEAD :].reshape(count, KV_HEADS, HEAD)
    scores = jnp.einsum(
        "pgrd,kgd->grpk", q_heads, k_heads, preferred_element_type=jnp.float32
    ) / jnp.sqrt(jnp.float32(HEAD))
    top = jnp.max(scores, axis=-1, keepdims=True)
    expo = jnp.exp(scores - top)
    weights = (expo / jnp.sum(expo, axis=-1, keepdims=True)).astype(jnp.bfloat16)
    out = jnp.einsum("grpk,kgd->pgrd", weights, v_heads, preferred_element_type=jnp.float32)
    return out.reshape(patches, HEADS * HEAD).astype(jnp.bfloat16)


def body(
    frames,
    gain_time,
    wq_time,
    wkv_time,
    wo_time,
    gain_space,
    wq_space,
    wkv_space,
    wo_space,
    gain_mlp,
    w_in,
    w_out,
):
    count = frames.shape[0]
    normed = layer_norm(frames, gain_time)
    queries = project(normed, wq_time).astype(jnp.bfloat16)
    keyvals = project(normed, wkv_time).astype(jnp.bfloat16)
    padded = extended(keyvals, (("tm", 0),), WINDOW)
    extent = padded.shape[0]
    first = lax.axis_index("tm") * count
    total = count * lax.axis_size("tm")
    query_pos = jnp.arange(count, dtype=jnp.int32)[:, None]
    key_pos = jnp.arange(extent, dtype=jnp.int32)[None, :] - WINDOW
    global_key = first + key_pos
    valid = (jnp.abs(key_pos - query_pos) <= WINDOW) & (global_key >= 0) & (global_key < total)
    attended = banded_time(queries, padded, valid)
    after_time = (frames.astype(jnp.float32) + project(attended, wo_time)).astype(jnp.bfloat16)
    normed = layer_norm(after_time, gain_space)
    queries = project(normed, wq_space).astype(jnp.bfloat16)
    keyvals = project(normed, wkv_space).astype(jnp.bfloat16)
    gathered = lax.all_gather(keyvals, "space", axis=1, tiled=True)
    attended = jax.vmap(attend_space)(queries, gathered)
    after_space = (after_time.astype(jnp.float32) + project(attended, wo_space)).astype(
        jnp.bfloat16
    )
    normed = layer_norm(after_space, gain_mlp)
    hidden = jax.nn.gelu(project(normed, w_in), approximate=True).astype(jnp.bfloat16)
    return (after_space.astype(jnp.float32) + project(hidden, w_out)).astype(jnp.bfloat16)


def solution(mesh):
    in_specs = (P("tm", "space", None), P(), P(), P(), P(), P(), P(), P(), P(), P(), P(), P())
    out_specs = P("tm", "space", None)
    return jax.shard_map(body, mesh=mesh, in_specs=in_specs, out_specs=out_specs, check_vma=False)
```

profile of v0, /device:TPU:0, one launch (start us, length us, event | category | flops | bytes accessed | tf_op | source)
XLA Modules:
  0.0 242.6 jit_solution(12706470925719395757)
XLA Ops:
  6.5 0.0 copy-start
  6.5 0.0 copy-start.2
  6.5 0.0 all-gather.2.cloned.1.call-start
  6.6 1.8 convert_reduce_fusion.2
  8.4 2.0 fusion.35
  10.4 0.0 copy-done.2
  10.4 0.0 copy-done.14
  10.4 0.0 copy-done.12
  10.5 0.0 copy-start.11
  10.5 1.0 convolution_convert_fusion.3
  11.5 0.0 copy-start.7
  11.5 1.0 copy-done.7
  12.5 0.9 fusion.100
  13.4 3.2 %collective-permute-start = (bf16[8,64,512]{2,1,0:T(8,128)(2,1)}, bf16[8,64,512]{2,1,0:T(8,128)(2,1)}, u32[]{:S(2)}, u32[]{:S(2)}) collective-permute-start(bf16[8,64,512]{2,1,0:T(8,128)(2,1)} %get-tuple-element.9), channel_id=1, source_target_pairs={{0,4},{4,8},{8,12},{12,16},{16,20},{20,24},{24,28},{1,5},{5,9},{9,... | collective-permute-start | bytes 1572872 | tf_op jit(solution)/shard_map/ppermute | solution.py:19
  16.5 1.3 collective-permute-start.1
  17.8 0.0 copy-done.11
  17.8 2.7 %convolution_convert_fusion.1 = bf16[16,64,768]{2,1,0:T(8,128)(2,1)} fusion(bf16[768,768]{1,0:T(8,128)(2,1)S(1)} %copy-done.11, bf16[16,64,768]{2,1,0:T(8,128)(2,1)S(1)} %copy-done.2, f32[768]{0:T(1024)S(1)} %copy-done.14, f32[16,64]{1,0:T(8,128)S(1)} %add_rsqrt_fusion.2, f32[16,64]{1,0:T(8,128)S(1)} %broadcast_multiply_fusion.2), kind=kOutput, calls=%fused_computation.69 | convolution fusion | flops 1212678144 | bytes 4336640 | tf_op jit(solution)/shard_map/dot_general | solution.py:34
  20.5 9.1 %reshape.113 = bf16[16,64,4,3,64]{4,3,2,1,0:T(4,128)(2,1)} reshape(bf16[16,64,768]{2,1,0:T(8,128)(2,1)} %convolution_convert_fusion.1) | data formatting | bytes 3145728 | tf_op jit(solution)/shard_map/reshape | solution.py:44
  29.6 0.0 collective-permute-done
  29.7 0.0 collective-permute-done.1
  29.7 0.0 copy-done.8
  29.7 1.4 pad_maximum_fusion
  31.1 1.2 fusion.99
  32.4 1.8 reshape.112
  34.2 3.3 %reshape.114 = bf16[32,64,4,64]{3,2,1,0:T(4,128)(2,1)S(1)} reshape(bf16[32,64,256]{2,1,0:T(8,128)(2,1)} %get-tuple-element.8) | data formatting | bytes 2097152 | tf_op jit(solution)/shard_map/reshape | solution.py:45
  37.5 5.9 %fusion.44 = f32[64,4,16,3,32]{4,2,3,1,0:T(8,128)S(1)} fusion(bf16[16,64,4,3,64]{4,3,2,1,0:T(4,128)(2,1)} %reshape.113, bf16[32,64,4,64,1]{3,2,1,0,4:T(4,128)(2,1)S(1)} %bitcast.75), kind=kOutput, calls=%fused_computation.57 | convolution fusion | flops 50331648 | bytes 4194304 | tf_op jit(solution)/shard_map/tpgrd,spgd->pgtrs/dot_general | solution.py:47
  43.4 4.3 %fusion.101 = (f32[64,4,16,3]{2,3,1,0:T(4,128)S(1)}, f32[64,4,16,3,32]{4,2,3,1,0:T(8,128)S(1)}) fusion(f32[64,4,16,3,32]{4,2,3,1,0:T(8,128)S(1)} %fusion.44, pred[16,32]{1,0:T(8,128)(4,1)S(1)} %fusion.87), kind=kOutput, calls=%fused_computation.105 | output fusion | flops 2359327 | bytes 3195392 | tf_op jit(solution)/shard_map/sub | solution.py:52
  47.7 0.0 copy-done.9
  47.7 2.9 %convert_bitcast_fusion = bf16[16,64,4,3,64]{4,0,3,2,1:T(8,128)(2,1)S(1)} fusion(f32[64,4,16,3,32]{4,2,3,1,0:T(8,128)S(1)} %get-tuple-element.12, f32[64,4,16,3]{2,3,1,0:T(4,128)S(1)} %get-tuple-element.11, bf16[32,64,4,64,1]{3,2,1,0,4:T(4,128)(2,1)S(1)} %bitcast.77), kind=kOutput, calls=%fused_computation.59 | convolution fusion | flops 51904512 | bytes 4243456 | tf_op jit(solution)/shard_map/pgtrs,spgd->tpgrd/dot_general | solution.py:54
  50.6 3.8 %copy.23 = bf16[16,64,4,3,64]{4,3,2,1,0:T(4,128)(2,1)} copy(bf16[16,64,4,3,64]{4,0,3,2,1:T(8,128)(2,1)S(1)} %convert_bitcast_fusion) | data formatting | bytes 3145728 | tf_op jit(solution)/shard_map/convert_element_type | solution.py:55
  54.5 8.3 %convert_element_type.80 = bf16[16,64,768]{2,1,0:T(8,128)(2,1)} reshape(bf16[16,64,4,3,64]{4,3,2,1,0:T(4,128)(2,1)} %copy.23) | data formatting | bytes 3145728 | tf_op jit(solution)/shard_map/convert_element_type | solution.py:55
  62.8 0.0 copy-done
  62.8 0.0 copy-done.3
  62.8 0.0 copy-start.15
  62.8 2.9 %convert_reduce_fusion.1 = (f32[16,64]{1,0:T(8,128)S(1)}, bf16[16,64,768]{2,1,0:T(8,128)(2,1)S(1)}) fusion(bf16[16,64,768]{2,1,0:T(8,128)(2,1)} %convert_element_type.80, bf16[768,768]{1,0:T(8,128)(2,1)S(1)} %copy-done, bf16[16,64,768]{2,1,0:T(8,128)(2,1)S(1)} %copy-done.3), kind=kOutput, calls=%fused_computation.29 | convolution fusion | flops 1211890688 | bytes 5902336 | tf_op jit(solution)/shard_map/dot_general | solution.py:34
  65.8 0.0 copy-start.4
  65.8 0.6 fusion.32
  66.4 0.5 copy-done.4
  66.9 0.0 copy-done.13
  66.9 0.0 copy-done.15
  66.9 2.0 convolution_convert_fusion.2
  69.0 0.0 all-gather.2.cloned.1.call-update
  69.0 3.3 %convolution_convert_fusion = bf16[16,64,768]{2,1,0:T(8,128)(2,1)S(1)} fusion(bf16[768,768]{1,0:T(8,128)(2,1)} %param.18, bf16[16,64,768]{2,1,0:T(8,128)(2,1)} %copy-done.4, f32[768]{0:T(1024)S(1)} %copy-done.15, f32[16,64]{1,0:T(8,128)S(1)} %add_rsqrt_fusion.1, f32[16,64]{1,0:T(8,128)S(1)} %broadcast_multiply_fusion.1), kind=kOutput, calls=%fused_computation.68 | convolution fusion | flops 1212678144 | bytes 4336640 | tf_op jit(solution)/shard_map/dot_general | solution.py:34
  72.3 5.0 %reshape.117 = bf16[16,64,4,3,64]{4,3,2,1,0:T(4,128)(2,1)} reshape(bf16[16,64,768]{2,1,0:T(8,128)(2,1)S(1)} %convolution_convert_fusion) | data formatting | bytes 3145728 | tf_op jit(solution)/shard_map/vmap()/reshape | solution.py:62
  77.2 76.5 %all-gather.2.cloned.1.call-done = bf16[16,256,512]{2,1,0:T(8,128)(2,1)} async-done(((bf16[16,64,512]{2,1,0:T(8,128)(2,1)}), bf16[16,256,512]{2,1,0:T(8,128)(2,1)}) %all-gather.2.cloned.1.call-update) | async-done | bytes 4194320 | tf_op jit(solution)/shard_map/all_gather | solution.py:106
  153.7 4.6 %fusion.98 = (bf16[16,256,256]{2,1,0:T(8,128)(2,1)}, bf16[16,256,256]{2,1,0:T(8,128)(2,1)}) fusion(bf16[16,256,512]{2,1,0:T(8,128)(2,1)} %all-gather.2.cloned.1.call-done), kind=kLoop, calls=%fused_computation.102 | loop fusion | bytes 8388608 | tf_op jit(solution)/shard_map/vmap()/slice | solution.py:63
  158.4 2.8 %copy.25 = bf16[16,256,256]{1,2,0:T(8,128)(2,1)S(1)} copy(bf16[16,256,256]{2,1,0:T(8,128)(2,1)} %get-tuple-element.5) | data formatting | bytes 4194304 | tf_op jit(solution)/shard_map/vmap()/slice | solution.py:63
  161.2 4.1 %copy.24 = bf16[16,256,256]{1,2,0:T(8,128)(2,1)} copy(bf16[16,256,256]{2,1,0:T(8,128)(2,1)} %get-tuple-element.6) | data formatting | bytes 4194304 | tf_op jit(solution)/shard_map/vmap()/slice | solution.py:64
  165.3 8.5 %fusion.42 = f32[16,4,256,64,3]{2,3,4,1,0:T(8,128)} fusion(bf16[16,256,4,64,1]{1,3,4,2,0:T(8,128)(2,1)S(1)} %bitcast.74, bf16[16,64,4,3,64]{4,3,2,1,0:T(4,128)(2,1)} %reshape.117), kind=kOutput, calls=%fused_computation.55 | convolution fusion | flops 402653184 | bytes 16252928 | tf_op jit(solution)/shard_map/vmap(pgrd,kgd->grpk)/dot_general | solution.py:65
  173.9 12.9 %fusion.102 = f32[16,4,3,64]{3,2,1,0:T(4,128)S(1)} fusion(f32[16,4,256,64,3]{2,3,4,1,0:T(8,128)} %fusion.42), kind=kOutput, calls=%fused_computation.106 | output fusion | flops 12583167 | bytes 12632064 | tf_op jit(solution)/shard_map/vmap()/sub | solution.py:69
  186.8 0.0 copy-start.5
  186.8 0.0 copy-start.10
  186.8 27.2 %fusion.50 = bf16[16,4,64,3,64]{4,2,3,1,0:T(8,128)(2,1)} fusion(bf16[16,256,4,64,1]{1,3,4,2,0:T(8,128)(2,1)} %bitcast.78, f32[16,4,3,64]{3,2,1,0:T(4,128)S(1)} %fusion.102, f32[16,4,256,64,3]{2,3,4,1,0:T(8,128)} %fusion.42), kind=kOutput, calls=%fused_computation.64 | convolution fusion | flops 419180800 | bytes 16302080 | tf_op jit(solution)/shard_map/vmap(grpk,kgd->pgrd)/dot_general | solution.py:71
  214.0 0.0 copy-done.5
  214.0 0.0 copy-done.10
  214.0 0.0 copy-start.16
  214.0 3.6 %convert_reduce_fusion = (f32[16,64]{1,0:T(8,128)S(1)}, bf16[16,64,768]{2,1,0:T(8,128)(2,1)S(1)}) fusion(bf16[16,64,768]{1,2,0:T(8,128)(2,1)} %bitcast.76, bf16[768,768]{1,0:T(8,128)(2,1)S(1)} %copy-done.10, bf16[16,64,768]{2,1,0:T(8,128)(2,1)S(1)} %copy-done.5), kind=kOutput, calls=%fused_computation.26 | convolution fusion | flops 1211890688 | bytes 5902336 | tf_op jit(solution)/shard_map/dot_general | solution.py:34
  217.6 0.0 copy-start.6
  217.6 1.1 copy-done.6
  218.7 0.6 fusion.29
  219.3 0.0 copy-done.16
  219.3 0.0 copy-start.1
  219.3 16.2 %fusion.40 = bf16[16,64,768]{2,1,0:T(8,128)(2,1)} fusion(bf16[16,64,768]{2,1,0:T(8,128)(2,1)} %copy-done.6, bf16[3072,768]{1,0:T(8,128)(2,1)} %param.23, bf16[768,3072]{1,0:T(8,128)(2,1)} %param.22, f32[768]{0:T(1024)S(1)} %copy-done.16, f32[16,64]{1,0:T(8,128)S(1)} %add_rsqrt_fusion, f32[16,64]{1,0:T(8,128)S(1)} %broadcast_multiply_fusion), kind=kOutput, calls=%fused_computation.53 | convolution fusion | flops 9698279424 | bytes 12594176 | tf_op jit(solution)/shard_map/dot_general | solution.py:34
  235.6 0.0 copy-done.1
  (15 shorter events, 0.1 us)
Async XLA Ops:
  6.5 56.3 %copy-start = (bf16[768,768]{1,0:T(8,128)(2,1)S(1)}, bf16[768,768]{1,0:T(8,128)(2,1)}, u32[]{:S(2)}) copy-start(bf16[768,768]{1,0:T(8,128)(2,1)} %param.16) | copy-start | bytes 3538948
  6.5 3.9 %copy-start.2 = (bf16[16,64,768]{2,1,0:T(8,128)(2,1)S(1)}, bf16[16,64,768]{2,1,0:T(8,128)(2,1)}, u32[]{:S(2)}) copy-start(bf16[16,64,768]{2,1,0:T(8,128)(2,1)} %param.12) | copy-start | bytes 4718596
  6.5 3.9 %copy-start.14 = (f32[768]{0:T(1024)S(1)}, f32[768]{0:T(1024)}, u32[]{:S(2)}) copy-start(f32[768]{0:T(1024)} %param.13) | copy-start | bytes 9220
  6.5 3.9 %copy-start.12 = (bf16[768,512]{1,0:T(8,128)(2,1)S(1)}, bf16[768,512]{1,0:T(8,128)(2,1)}, u32[]{:S(2)}) copy-start(bf16[768,512]{1,0:T(8,128)(2,1)} %param.15) | copy-start | bytes 2359300
  6.5 147.2 %all-gather.2.cloned.1.call-start = ((), (), s32[]{:S(2)}) async-start(), calls=%async_computation | async-start | bytes 5242880 | tf_op jit(solution)/shard_map/all_gather | solution.py:106
  10.5 7.4 %copy-start.11 = (bf16[768,768]{1,0:T(8,128)(2,1)S(1)}, bf16[768,768]{1,0:T(8,128)(2,1)}, u32[]{:S(2)}) copy-start(bf16[768,768]{1,0:T(8,128)(2,1)} %param.14) | copy-start | bytes 3538948
  11.5 1.0 copy-start.7
  13.4 16.3 %collective-permute-start = (bf16[8,64,512]{2,1,0:T(8,128)(2,1)}, bf16[8,64,512]{2,1,0:T(8,128)(2,1)}, u32[]{:S(2)}, u32[]{:S(2)}) collective-permute-start(bf16[8,64,512]{2,1,0:T(8,128)(2,1)} %get-tuple-element.9), channel_id=1, source_target_pairs={{0,4},{4,8},{8,12},{12,16},{16,20},{20,24},{24,28},{1,5},{5,9},{9,... | collective-permute-start | bytes 1572872 | tf_op jit(solution)/shard_map/ppermute | solution.py:19
  16.5 13.1 %collective-permute-start.1 = (bf16[8,64,512]{2,1,0:T(8,128)(2,1)S(1)}, bf16[8,64,512]{2,1,0:T(8,128)(2,1)}, u32[]{:S(2)}, u32[]{:S(2)}) collective-permute-start(bf16[8,64,512]{2,1,0:T(8,128)(2,1)S(1)} %get-tuple-element.10), channel_id=1, source_target_pairs={{4,0},{8,4},{12,8},{16,12},{20,16},{24,20},{28,24},{5,1},{9,5},{13... | collective-permute-start | bytes 1572872 | tf_op jit(solution)/shard_map/ppermute | solution.py:20
  20.5 9.1 %copy-start.8 = (bf16[16,64,512]{2,1,0:T(8,128)(2,1)S(1)}, bf16[16,64,512]{2,1,0:T(8,128)(2,1)}, u32[]{:S(2)}) copy-start(bf16[16,64,512]{2,1,0:T(8,128)(2,1)} %copy-done.7) | copy-start | bytes 3145732
  43.4 4.3 %copy-start.9 = (bf16[32,64,4,64]{3,2,1,0:T(4,128)(2,1)S(1)}, bf16[32,64,4,64]{3,2,1,0:T(4,128)(2,1)}, u32[]{:S(2)}) copy-start(bf16[32,64,4,64]{3,2,1,0:T(4,128)(2,1)} %reshape.112) | copy-start | bytes 3145732
  54.5 8.4 %copy-start.3 = (bf16[16,64,768]{2,1,0:T(8,128)(2,1)S(1)}, bf16[16,64,768]{2,1,0:T(8,128)(2,1)}, u32[]{:S(2)}) copy-start(bf16[16,64,768]{2,1,0:T(8,128)(2,1)} %param.12) | copy-start | bytes 4718596
  62.8 4.1 %copy-start.13 = (bf16[768,512]{1,0:T(8,128)(2,1)S(1)}, bf16[768,512]{1,0:T(8,128)(2,1)}, u32[]{:S(2)}) copy-start(bf16[768,512]{1,0:T(8,128)(2,1)} %param.19) | copy-start | bytes 2359300
  62.8 4.1 %copy-start.15 = (f32[768]{0:T(1024)S(1)}, f32[768]{0:T(1024)}, u32[]{:S(2)}) copy-start(f32[768]{0:T(1024)} %param.17) | copy-start | bytes 9220
  65.8 1.1 copy-start.4
  186.8 27.2 %copy-start.5 = (bf16[16,64,768]{2,1,0:T(8,128)(2,1)S(1)}, bf16[16,64,768]{2,1,0:T(8,128)(2,1)}, u32[]{:S(2)}) copy-start(bf16[16,64,768]{2,1,0:T(8,128)(2,1)} %copy-done.4) | copy-start | bytes 4718596
  186.8 27.2 %copy-start.10 = (bf16[768,768]{1,0:T(8,128)(2,1)S(1)}, bf16[768,768]{1,0:T(8,128)(2,1)}, u32[]{:S(2)}) copy-start(bf16[768,768]{1,0:T(8,128)(2,1)} %param.20) | copy-start | bytes 3538948
  214.0 5.3 %copy-start.16 = (f32[768]{0:T(1024)S(1)}, f32[768]{0:T(1024)}, u32[]{:S(2)}) copy-start(f32[768]{0:T(1024)} %param.21) | copy-start | bytes 9220
  217.6 1.2 copy-start.6
  219.3 16.2 %copy-start.1 = (bf16[768,768]{1,0:T(8,128)(2,1)S(1)}, bf16[768,768]{1,0:T(8,128)(2,1)}, u32[]{:S(2)}) copy-start(bf16[768,768]{1,0:T(8,128)(2,1)} %param.16) | copy-start | bytes 3538948
Sparse Core Ops, SparseCore 0:
  69.1 84.5 all-gather.1
where the time goes:
time: 247 us; the launch traced here: 243 us
  waiting for transfers between devices  76.5 us (31%)
  matrix products  76.3 us (31%)
  local copies, waits for them, and re-layouts  47.8 us (19%)
  other arithmetic  23.6 us (10%)
  between operations  14 us (6%)
  starting transfers between devices  4.47 us (2%)
    all_gather x1, waiting for transfers between devices, body(): gathered = lax.all_gather(keyvals, 'space', axis=1, tiled=True)  76.5 us
    dot_general x7, matrix products, project(): jnp.dot(flat, w, preferred_element_type=jnp.float32)  31.7 us
    dot_general x1, matrix products, attend_space(): jnp.einsum('grpk,kgd->pgrd', weights, v_heads, preferred_element_type=jnp...  27.2 us
    sub x1, other arithmetic, attend_space(): expo = jnp.exp(scores - top)  12.9 us
    convert_element_type x2, local copies, waits for them, and re-layouts, banded_time(): return out.reshape(count, patches, HEADS * HEAD).astype(jnp.bfloat16)  12.2 us
    reshape x1, local copies, waits for them, and re-layouts, banded_time(): q_heads = queries.reshape(count, patches, KV_HEADS, group, HEAD)  9.09 us
    dot_general x1, matrix products, attend_space(): jnp.einsum('pgrd,kgd->grpk', q_heads, k_heads, preferred_element_type=jnp...  8.54 us
    slice x2, local copies, waits for them, and re-layouts, attend_space(): k_heads = keyvals[:, :KV_HEADS * HEAD].reshape(count, KV_HEADS, HEAD)  7.49 us
  transfers between devices with their start and end apart: 3, of which 1 were waited for; matrix products, arithmetic and copies ran while one was open for 8% of the time, Pallas kernels for 0%

commit v1 on v0

--- a/solution.py
+++ b/solution.py
@@ -103,7 +103,25 @@
     normed = layer_norm(after_time, gain_space)
     queries = project(normed, wq_space).astype(jnp.bfloat16)
     keyvals = project(normed, wkv_space).astype(jnp.bfloat16)
-    gathered = lax.all_gather(keyvals, "space", axis=1, tiled=True)
+    n_now, arr_next, low = (lax.psum(1, "space"), lax.axis_index("space"), keyvals.shape[1])
+    xs_all = tuple(((no, (no + 1) % n_now) for no in range(n_now)))
+    gathered = jnp.zeros((*keyvals.shape[:1], n_now * low, *keyvals.shape[2:]), keyvals.dtype)
+    gathered = lax.dynamic_update_slice_in_dim(gathered, keyvals, arr_next * low, axis=1)
+    y2 = z2 = keyvals
+    answer = n_now // 2
+    so_far_all = tuple(((no, (no - 1) % n_now) for no in range(n_now)))
+    rr = 1
+    while rr < answer + 1:
+        y2 = lax.ppermute(y2, "space", perm=xs_all)
+        gathered = lax.dynamic_update_slice_in_dim(
+            gathered, y2, (arr_next - rr) % n_now * low, axis=1
+        )
+        if rr < n_now - answer:
+            z2 = lax.ppermute(z2, "space", so_far_all)
+            gathered = lax.dynamic_update_slice_in_dim(
+                gathered, z2, (arr_next + rr) % n_now * low, axis=1
+            )
+        rr += 1
     attended = jax.vmap(attend_space)(queries, gathered)
     after_space = (after_time.astype(jnp.float32) + project(attended, wo_space)).astype(
         jnp.bfloat16

time: 247 us -> 294 us (1.19)
  the two profiles are of different devices: /device:TPU:0 before, /device:TPU:20 now
where the time goes in v1:
time: 294 us; the launch traced here: 288 us
  local copies, waits for them, and re-layouts  134 us (46%)
  matrix products  74.9 us (25%)
  waiting for transfers between devices  46.3 us (16%)
  other arithmetic  23.6 us (8%)
  starting transfers between devices  8.44 us (3%)
    ppermute x2, waiting for transfers between devices, body(): y2 = lax.ppermute(y2, 'space', perm=xs_all)  46.3 us
    dynamic_update_slice x2, local copies, waits for them, and re-layouts, body(): lax.dynamic_update_slice_in_dim(gathered, y2, (arr_next - rr) % n_now * l...  41.4 us
    dot_general x7, matrix products, project(): jnp.dot(flat, w, preferred_element_type=jnp.float32)  33 us
    dot_general x1, matrix products, attend_space(): jnp.einsum('grpk,kgd->pgrd', weights, v_heads, preferred_element_type=jnp...  27.1 us
    dynamic_update_slice x1, local copies, waits for them, and re-layouts, body(): lax.dynamic_update_slice_in_dim(gathered, z2, (arr_next + rr) % n_now * l...  21 us
    dynamic_update_slice x1, local copies, waits for them, and re-layouts, body(): lax.dynamic_update_slice_in_dim(gathered, keyvals, arr_next * low, axis=1)  17.7 us
    sub x1, other arithmetic, attend_space(): expo = jnp.exp(scores - top)  12.9 us
    convert_element_type x2, local copies, waits for them, and re-layouts, banded_time(): return out.reshape(count, patches, HEADS * HEAD).astype(jnp.bfloat16)  12.2 us
  transfers between devices with their start and end apart: 5, of which 1 were waited for; matrix products, arithmetic and copies ran while one was open for 32% of the time, Pallas kernels for 0%

profile of v1, /device:TPU:20, one launch (start us, length us, event | category | flops | bytes accessed | tf_op | source)
XLA Modules:
  0.0 288.0 jit_solution(17521925085515673007)
XLA Ops:
  0.0 0.0 copy-start
  0.0 0.0 copy-start.11
  0.0 1.8 convert_reduce_fusion.2
  1.9 2.0 fusion.35
  3.9 0.0 copy-done.3
  3.9 0.0 copy-done.13
  3.9 0.0 copy-done.11
  3.9 0.0 copy-start.10
  3.9 1.0 convolution_convert_fusion.3
  5.0 0.1 fusion.100
  5.1 2.8 collective-permute-start.1
  7.8 1.9 collective-permute-start
  9.8 0.0 copy-done.10
  9.8 2.7 convolution_convert_fusion.1
  12.5 8.9 %reshape.113 = bf16[16,64,4,3,64]{4,3,2,1,0:T(4,128)(2,1)} reshape(bf16[16,64,768]{2,1,0:T(8,128)(2,1)} %convolution_convert_fusion.1) | data formatting | bytes 3145728 | tf_op jit(solution)/shard_map/reshape | solution.py:44
  21.5 0.0 collective-permute-done.1
  21.5 0.0 collective-permute-done
  21.5 1.4 pad_maximum_fusion
  22.9 1.6 fusion.99
  24.5 3.3 %reshape.114 = bf16[32,64,4,64]{3,2,1,0:T(4,128)(2,1)S(1)} reshape(bf16[32,64,256]{2,1,0:T(8,128)(2,1)} %get-tuple-element.8) | data formatting | bytes 2097152 | tf_op jit(solution)/shard_map/reshape | solution.py:45
  27.9 4.4 %reshape.112 = bf16[32,64,4,64]{3,2,1,0:T(4,128)(2,1)} reshape(bf16[32,64,256]{2,1,0:T(8,128)(2,1)} %get-tuple-element.7) | data formatting | bytes 2097152 | tf_op jit(solution)/shard_map/reshape | solution.py:46
  32.3 5.9 %fusion.44 = f32[64,4,16,3,32]{4,2,3,1,0:T(8,128)S(1)} fusion(bf16[16,64,4,3,64]{4,3,2,1,0:T(4,128)(2,1)} %reshape.113, bf16[32,64,4,64,1]{3,2,1,0,4:T(4,128)(2,1)S(1)} %bitcast.75), kind=kOutput, calls=%fused_computation.57 | convolution fusion | flops 50331648 | bytes 4194304 | tf_op jit(solution)/shard_map/tpgrd,spgd->pgtrs/dot_general | solution.py:47
  38.2 4.3 %fusion.101 = (f32[64,4,16,3]{2,3,1,0:T(4,128)S(1)}, f32[64,4,16,3,32]{4,2,3,1,0:T(8,128)S(1)}) fusion(f32[64,4,16,3,32]{4,2,3,1,0:T(8,128)S(1)} %fusion.44, pred[16,32]{1,0:T(8,128)(4,1)S(1)} %fusion.87), kind=kOutput, calls=%fused_computation.105 | output fusion | flops 2359327 | bytes 3195392 | tf_op jit(solution)/shard_map/sub | solution.py:52
  42.5 0.0 copy-done.8
  42.5 2.6 convert_bitcast_fusion
  45.1 3.8 %copy.25 = bf16[16,64,4,3,64]{4,3,2,1,0:T(4,128)(2,1)} copy(bf16[16,64,4,3,64]{4,0,3,2,1:T(8,128)(2,1)S(1)} %convert_bitcast_fusion) | data formatting | bytes 3145728 | tf_op jit(solution)/shard_map/convert_element_type | solution.py:55
  48.9 8.3 %convert_element_type.80 = bf16[16,64,768]{2,1,0:T(8,128)(2,1)} reshape(bf16[16,64,4,3,64]{4,3,2,1,0:T(4,128)(2,1)} %copy.25) | data formatting | bytes 3145728 | tf_op jit(solution)/shard_map/convert_element_type | solution.py:55
  57.3 0.0 copy-done
  57.3 0.0 copy-done.4
  57.3 0.0 copy-start.14
  57.3 2.9 %convert_reduce_fusion.1 = (f32[16,64]{1,0:T(8,128)S(1)}, bf16[16,64,768]{2,1,0:T(8,128)(2,1)S(1)}) fusion(bf16[16,64,768]{2,1,0:T(8,128)(2,1)} %convert_element_type.80, bf16[768,768]{1,0:T(8,128)(2,1)S(1)} %copy-done, bf16[16,64,768]{2,1,0:T(8,128)(2,1)S(1)} %copy-done.4), kind=kOutput, calls=%fused_computation.29 | convolution fusion | flops 1211890688 | bytes 5902336 | tf_op jit(solution)/shard_map/dot_general | solution.py:34
  60.3 0.0 copy-start.5
  60.3 0.6 fusion.32
  60.9 2.0 convolution_convert_fusion.2
  62.9 0.0 copy-done.5
  62.9 1.6 collective-permute-start.2
  64.5 0.4 collective-permute-start.3
  64.9 46.3 %collective-permute-done.2 = bf16[16,64,512]{2,1,0:T(8,128)(2,1)S(1)} collective-permute-done((bf16[16,64,512]{2,1,0:T(8,128)(2,1)}, bf16[16,64,512]{2,1,0:T(8,128)(2,1)S(1)}, u32[]{:S(2)}, u32[]{:S(2)}) %collective-permute-start.2) | collective-permute-done | bytes 1048608 | tf_op jit(solution)/shard_map/ppermute | solution.py:115
  111.2 1.7 collective-permute-start.4
  112.9 2.0 copy.26
  114.9 4.4 %convolution_convert_fusion = bf16[16,64,768]{2,1,0:T(8,128)(2,1)} fusion(bf16[768,768]{1,0:T(8,128)(2,1)} %param.18, bf16[16,64,768]{2,1,0:T(8,128)(2,1)} %copy-done.5, f32[768]{0:T(1024)S(1)} %copy-done.14, f32[16,64]{1,0:T(8,128)S(1)} %add_rsqrt_fusion.1, f32[16,64]{1,0:T(8,128)S(1)} %broadcast_multiply_fusion.1), kind=kOutput, calls=%fused_computation.68 | convolution fusion | flops 1212678144 | bytes 4336640 | tf_op jit(solution)/shard_map/dot_general | solution.py:34
  119.4 8.8 %reshape.117 = bf16[16,64,4,3,64]{4,3,2,1,0:T(4,128)(2,1)} reshape(bf16[16,64,768]{2,1,0:T(8,128)(2,1)} %convolution_convert_fusion) | data formatting | bytes 3145728 | tf_op jit(solution)/shard_map/vmap()/reshape | solution.py:62
  128.2 2.4 broadcast_in_dim.16
  130.5 17.7 %dynamic_update_slice.12 = bf16[16,256,512]{1,2,0:T(8,128)(2,1)} dynamic-update-slice(bf16[16,256,512]{1,2,0:T(8,128)(2,1)} %broadcast_in_dim.16, bf16[16,64,512]{1,2,0:T(8,128)(2,1)S(1)} %copy.26, s32[]{:T(128)} %constant.65.clone.1, s32[]{:T(128)S(6)} %select_n.32, s32[]{:T(128)} %constant.65.clone.1) | dynamic-update-slice | bytes 2097156 | tf_op jit(solution)/shard_map/dynamic_update_slice | solution.py:109
  148.2 1.1 copy.27
  149.3 21.9 %dynamic_update_slice.13 = bf16[16,256,512]{1,2,0:T(8,128)(2,1)} dynamic-update-slice(bf16[16,256,512]{1,2,0:T(8,128)(2,1)} %dynamic_update_slice.12, bf16[16,64,512]{1,2,0:T(8,128)(2,1)S(1)} %copy.27, s32[]{:T(128)} %constant.65.clone.1, s32[]{:T(128)S(6)} %select_n.34, s32[]{:T(128)} %constant.65.clone.1) | dynamic-update-slice | bytes 2097156 | tf_op jit(solution)/shard_map/dynamic_update_slice | solution.py:116
  171.2 0.0 collective-permute-done.3
  171.2 2.0 copy.28
  173.2 21.0 %dynamic_update_slice.14 = bf16[16,256,512]{1,2,0:T(8,128)(2,1)} dynamic-update-slice(bf16[16,256,512]{1,2,0:T(8,128)(2,1)} %dynamic_update_slice.13, bf16[16,64,512]{1,2,0:T(8,128)(2,1)S(1)} %copy.28, s32[]{:T(128)} %constant.65.clone.1, s32[]{:T(128)S(6)} %select_n.36, s32[]{:T(128)} %constant.65.clone.1) | dynamic-update-slice | bytes 2097156 | tf_op jit(solution)/shard_map/dynamic_update_slice | solution.py:121
  194.3 0.0 collective-permute-done.4
  194.3 2.0 copy.29
  196.3 19.4 %dynamic_update_slice.15 = bf16[16,256,512]{1,2,0:T(8,128)(2,1)} dynamic-update-slice(bf16[16,256,512]{1,2,0:T(8,128)(2,1)} %dynamic_update_slice.14, bf16[16,64,512]{1,2,0:T(8,128)(2,1)S(1)} %copy.29, s32[]{:T(128)} %constant.65.clone.1, s32[]{:T(128)S(6)} %select_n.38, s32[]{:T(128)} %constant.65.clone.1) | dynamic-update-slice | bytes 2097156 | tf_op jit(solution)/shard_map/dynamic_update_slice | solution.py:116
  215.8 4.1 %fusion.98 = (bf16[16,256,256]{1,2,0:T(8,128)(2,1)S(1)}, bf16[16,256,256]{1,2,0:T(8,128)(2,1)}) fusion(bf16[16,256,512]{1,2,0:T(8,128)(2,1)} %dynamic_update_slice.15), kind=kLoop, calls=%fused_computation.102 | loop fusion | bytes 8388608 | tf_op jit(solution)/shard_map/vmap()/slice | solution.py:63
  219.8 6.3 %fusion.42 = f32[16,4,256,64,3]{2,3,4,1,0:T(8,128)} fusion(bf16[16,256,4,64,1]{1,3,4,2,0:T(8,128)(2,1)S(1)} %bitcast.74, bf16[16,64,4,3,64]{4,3,2,1,0:T(4,128)(2,1)S(1)} %copy-done.2), kind=kOutput, calls=%fused_computation.55 | convolution fusion | flops 402653184 | bytes 16252928 | tf_op jit(solution)/shard_map/vmap(pgrd,kgd->grpk)/dot_general | solution.py:65
  226.2 12.9 %fusion.102 = f32[16,4,3,64]{3,2,1,0:T(4,128)S(1)} fusion(f32[16,4,256,64,3]{2,3,4,1,0:T(8,128)} %fusion.42), kind=kOutput, calls=%fused_computation.106 | output fusion | flops 12583167 | bytes 12632064 | tf_op jit(solution)/shard_map/vmap()/sub | solution.py:69
  239.0 0.0 copy-start.6
  239.0 0.0 copy-start.9
  239.1 27.1 %fusion.50 = bf16[16,4,64,3,64]{4,2,3,1,0:T(8,128)(2,1)} fusion(bf16[16,256,4,64,1]{1,3,4,2,0:T(8,128)(2,1)} %bitcast.78, f32[16,4,3,64]{3,2,1,0:T(4,128)S(1)} %fusion.102, f32[16,4,256,64,3]{2,3,4,1,0:T(8,128)} %fusion.42), kind=kOutput, calls=%fused_computation.64 | convolution fusion | flops 419180800 | bytes 16302080 | tf_op jit(solution)/shard_map/vmap(grpk,kgd->pgrd)/dot_general | solution.py:71
  266.2 0.0 copy-start.15
  266.2 3.6 %convert_reduce_fusion = (f32[16,64]{1,0:T(8,128)S(1)}, bf16[16,64,768]{2,1,0:T(8,128)(2,1)S(1)}) fusion(bf16[16,64,768]{1,2,0:T(8,128)(2,1)} %bitcast.76, bf16[768,768]{1,0:T(8,128)(2,1)S(1)} %copy-done.9, bf16[16,64,768]{2,1,0:T(8,128)(2,1)S(1)} %copy-done.6), kind=kOutput, calls=%fused_computation.26 | convolution fusion | flops 1211890688 | bytes 5902336 | tf_op jit(solution)/shard_map/dot_general | solution.py:34
  269.8 1.1 copy-done.7
  271.0 0.6 fusion.29
  271.6 0.0 copy-start.1
  271.6 16.2 %fusion.40 = bf16[16,64,768]{2,1,0:T(8,128)(2,1)} fusion(bf16[16,64,768]{2,1,0:T(8,128)(2,1)} %copy-done.7, bf16[3072,768]{1,0:T(8,128)(2,1)} %param.23, bf16[768,3072]{1,0:T(8,128)(2,1)} %param.22, f32[768]{0:T(1024)S(1)} %copy-done.15, f32[16,64]{1,0:T(8,128)S(1)} %add_rsqrt_fusion, f32[16,64]{1,0:T(8,128)S(1)} %broadcast_multiply_fusion), kind=kOutput, calls=%fused_computation.53 | convolution fusion | flops 9698279424 | bytes 12594176 | tf_op jit(solution)/shard_map/dot_general | solution.py:34
  (23 shorter events, 0.1 us)
Async XLA Ops:
  0.0 57.3 %copy-start = (bf16[768,768]{1,0:T(8,128)(2,1)S(1)}, bf16[768,768]{1,0:T(8,128)(2,1)}, u32[]{:S(2)}) copy-start(bf16[768,768]{1,0:T(8,128)(2,1)} %param.16) | copy-start | bytes 3538948
  0.0 3.9 %copy-start.3 = (bf16[16,64,768]{2,1,0:T(8,128)(2,1)S(1)}, bf16[16,64,768]{2,1,0:T(8,128)(2,1)}, u32[]{:S(2)}) copy-start(bf16[16,64,768]{2,1,0:T(8,128)(2,1)} %param.12) | copy-start | bytes 4718596
  0.0 3.9 %copy-start.13 = (f32[768]{0:T(1024)S(1)}, f32[768]{0:T(1024)}, u32[]{:S(2)}) copy-start(f32[768]{0:T(1024)} %param.13) | copy-start | bytes 9220
  0.0 3.9 %copy-start.11 = (bf16[768,512]{1,0:T(8,128)(2,1)S(1)}, bf16[768,512]{1,0:T(8,128)(2,1)}, u32[]{:S(2)}) copy-start(bf16[768,512]{1,0:T(8,128)(2,1)} %param.15) | copy-start | bytes 2359300
  3.9 5.9 %copy-start.10 = (bf16[768,768]{1,0:T(8,128)(2,1)S(1)}, bf16[768,768]{1,0:T(8,128)(2,1)}, u32[]{:S(2)}) copy-start(bf16[768,768]{1,0:T(8,128)(2,1)} %param.14) | copy-start | bytes 3538948
  5.1 16.4 %collective-permute-start.1 = (bf16[8,64,512]{2,1,0:T(8,128)(2,1)S(1)}, bf16[8,64,512]{2,1,0:T(8,128)(2,1)}, u32[]{:S(2)}, u32[]{:S(2)}) collective-permute-start(bf16[8,64,512]{2,1,0:T(8,128)(2,1)S(1)} %get-tuple-element.10), channel_id=1, source_target_pairs={{4,0},{8,4},{12,8},{16,12},{20,16},{24,20},{28,24},{5,1},{9,5},{13... | collective-permute-start | bytes 1572872 | tf_op jit(solution)/shard_map/ppermute | solution.py:20
  7.8 13.6 %collective-permute-start = (bf16[8,64,512]{2,1,0:T(8,128)(2,1)S(1)}, bf16[8,64,512]{2,1,0:T(8,128)(2,1)}, u32[]{:S(2)}, u32[]{:S(2)}) collective-permute-start(bf16[8,64,512]{2,1,0:T(8,128)(2,1)S(1)} %get-tuple-element.9), channel_id=1, source_target_pairs={{0,4},{4,8},{8,12},{12,16},{16,20},{20,24},{24,28},{1,5},{5,9},{9,... | collective-permute-start | bytes 1572872 | tf_op jit(solution)/shard_map/ppermute | solution.py:19
  38.2 4.3 %copy-start.8 = (bf16[32,64,4,64]{3,2,1,0:T(4,128)(2,1)S(1)}, bf16[32,64,4,64]{3,2,1,0:T(4,128)(2,1)}, u32[]{:S(2)}) copy-start(bf16[32,64,4,64]{3,2,1,0:T(4,128)(2,1)} %reshape.112) | copy-start | bytes 3145732
  48.9 8.4 %copy-start.4 = (bf16[16,64,768]{2,1,0:T(8,128)(2,1)S(1)}, bf16[16,64,768]{2,1,0:T(8,128)(2,1)}, u32[]{:S(2)}) copy-start(bf16[16,64,768]{2,1,0:T(8,128)(2,1)} %param.12) | copy-start | bytes 4718596
  57.3 3.6 %copy-start.12 = (bf16[768,512]{1,0:T(8,128)(2,1)S(1)}, bf16[768,512]{1,0:T(8,128)(2,1)}, u32[]{:S(2)}) copy-start(bf16[768,512]{1,0:T(8,128)(2,1)} %param.19) | copy-start | bytes 2359300
  57.3 3.6 %copy-start.14 = (f32[768]{0:T(1024)S(1)}, f32[768]{0:T(1024)}, u32[]{:S(2)}) copy-start(f32[768]{0:T(1024)} %param.17) | copy-start | bytes 9220
  60.3 2.7 copy-start.5
  62.9 48.3 %collective-permute-start.2 = (bf16[16,64,512]{2,1,0:T(8,128)(2,1)}, bf16[16,64,512]{2,1,0:T(8,128)(2,1)S(1)}, u32[]{:S(2)}, u32[]{:S(2)}) collective-permute-start(bf16[16,64,512]{2,1,0:T(8,128)(2,1)} %convolution_convert_fusion.2), channel_id=1, source_target_pairs={{0,1},{1,2},{2,3},{3,0},{4,5},{5,6},{6,7},{7,4},{8,9},{9,10},{10,1... | collective-permute-start | bytes 3145736 | tf_op jit(solution)/shard_map/ppermute | solution.py:115
  64.5 106.7 %collective-permute-start.3 = (bf16[16,64,512]{2,1,0:T(8,128)(2,1)}, bf16[16,64,512]{2,1,0:T(8,128)(2,1)}, u32[]{:S(2)}, u32[]{:S(2)}) collective-permute-start(bf16[16,64,512]{2,1,0:T(8,128)(2,1)} %convolution_convert_fusion.2), channel_id=1, source_target_pairs={{0,3},{1,0},{2,1},{3,2},{4,7},{5,4},{6,5},{7,6},{8,11},{9,8},{10,9... | collective-permute-start | bytes 3145736 | tf_op jit(solution)/shard_map/ppermute | solution.py:120
  111.2 83.1 %collective-permute-start.4 = (bf16[16,64,512]{2,1,0:T(8,128)(2,1)S(1)}, bf16[16,64,512]{2,1,0:T(8,128)(2,1)}, u32[]{:S(2)}, u32[]{:S(2)}) collective-permute-start(bf16[16,64,512]{2,1,0:T(8,128)(2,1)S(1)} %collective-permute-done.2), channel_id=1, source_target_pairs={{0,1},{1,2},{2,3},{3,0},{4,5},{5,6},{6,7},{7,4},{8,9},{9,10},{10,1... | collective-permute-start | bytes 3145736 | tf_op jit(solution)/shard_map/ppermute | solution.py:115
  215.7 4.1 %copy-start.2 = (bf16[16,64,4,3,64]{4,3,2,1,0:T(4,128)(2,1)S(1)}, bf16[16,64,4,3,64]{4,3,2,1,0:T(4,128)(2,1)}, u32[]{:S(2)}) copy-start(bf16[16,64,4,3,64]{4,3,2,1,0:T(4,128)(2,1)} %reshape.117) | copy-start | bytes 4718596
  239.0 27.2 %copy-start.6 = (bf16[16,64,768]{2,1,0:T(8,128)(2,1)S(1)}, bf16[16,64,768]{2,1,0:T(8,128)(2,1)}, u32[]{:S(2)}) copy-start(bf16[16,64,768]{2,1,0:T(8,128)(2,1)} %copy-done.5) | copy-start | bytes 4718596
  239.0 27.2 %copy-start.9 = (bf16[768,768]{1,0:T(8,128)(2,1)S(1)}, bf16[768,768]{1,0:T(8,128)(2,1)}, u32[]{:S(2)}) copy-start(bf16[768,768]{1,0:T(8,128)(2,1)} %param.20) | copy-start | bytes 3538948
  266.2 5.3 %copy-start.15 = (f32[768]{0:T(1024)S(1)}, f32[768]{0:T(1024)}, u32[]{:S(2)}) copy-start(f32[768]{0:T(1024)} %param.21) | copy-start | bytes 9220
  269.8 1.2 copy-start.7
  271.6 16.2 %copy-start.1 = (bf16[768,768]{1,0:T(8,128)(2,1)S(1)}, bf16[768,768]{1,0:T(8,128)(2,1)}, u32[]{:S(2)}) copy-start(bf16[768,768]{1,0:T(8,128)(2,1)} %param.16) | copy-start | bytes 3538948
